TPU v7x, 32 devices: a whole 2x2x4 slice. The times are simulated.
32 devices in a mesh: groups: 1, tok: 8 (over z, y), exp: 2 (over x), sub: 2 (over core).
Axes of the slice: x: 2, y: 2, z: 4, core: 2. Of those that a mesh axis runs over, the one named last changes fastest.
Arguments:
- query: bfloat16 [2, 2, 4, 4096], P(('groups', 'sub'), 'exp'), may hold values from -9 to 9, as said below
- key_cache_table: bfloat16 [2, 2, 4, 1024, 512], P(('groups', 'sub'), 'exp', None, 'tok'), may hold values from -9 to 9, as said below
- value_cache_table: bfloat16 [2, 2, 4, 1024, 512], P(('groups', 'sub'), 'exp', None, 'tok'), may hold values from -6 to 6
- latest_key: bfloat16 [2, 2, 4, 512], P(('groups', 'sub'), 'exp'), may hold values from -6 to 6
- latest_value: bfloat16 [2, 2, 4, 512], P(('groups', 'sub'), 'exp'), may hold values from -6 to 6
- lengths: int32 [2, 2, 4], P(('groups', 'sub'), 'exp'), may hold values from 2 to 1024, as said below
- resid: bfloat16 [2, 2, 4, 2048], P(('groups', 'sub'), 'exp', None, 'tok'), may hold values from -250 to 250
- norm_gain: float32 [2048], replicated, may hold values from 0.5 to 1.5
- out_weight: bfloat16 [4096, 2048], P('tok'), may hold values from -0.09375 to 0.09375
- expert_ids: int32 [2, 2, 4, 8], P('groups'), may hold values from 0 to 15, all different within a row; in each aligned block of 16 rows (0 to 15, 16 to 31, ..., all dimensions but the last counted through in order) at most 16 rows name the same one
- gate_weights: float32 [2, 2, 4, 8], P('groups'), may hold values from 0.05 to 0.35
- w_gate: bfloat16 [16, 2048, 768], P(('tok', 'sub'), None, 'exp'), may hold values from -0.125 to 0.125
- w_up: bfloat16 [16, 2048, 768], P(('tok', 'sub'), None, 'exp'), may hold values from -0.125 to 0.125
- w_down: bfloat16 [16, 768, 2048], P(('tok', 'sub'), 'exp'), may hold values from -0.21875 to 0.21875
Outputs:
- attention_out: float32 [2, 2, 4, 2048], P(('groups', 'sub'), 'exp', None, 'tok')
- expert_out: float32 [2, 2, 4, 2048], P('groups', None, None, ('tok', 'exp', 'sub'))
Inputs may be any that keep to these rules, and one draw needn't show every extreme that they name: `query`: most entries are of order one; some rows may align queries of the first key head's query heads with the keys at positions 0 and 1. `key_cache_table`: most entries are of order one. `lengths`: some row reaches 1024. `expert_ids`: each row names 8 different experts; over all 16 rows no expert is named by more than 16 rows, a bound that some block reaches.
All inputs are finite; a program needn't handle non-finite values.
Results may differ from a plain program's by a relative error of at most 0.013.
Values may be sent and summed in bfloat16 or wider, within the bound.
No kernel may reach another device: no remote copies, remote signals or barrier semaphores. Data moves between devices by JAX's collectives and lax.ppermute only.
A program may use at most 64 MiB of HBM per device.

v0:
```python
import jax
import jax.numpy as jnp
from jax import lax
from jax.sharding import PartitionSpec as P

D = 2048
QUERY_HEADS = 32
KEY_VALUE_HEADS = 4
HEAD_DIMENSION = 128
TOPK = 8


def slot_table(chosen_ids, chosen_gates, experts_all, slots_cap):
    expert_iota = lax.broadcasted_iota(jnp.int32, (1, 1, experts_all), 2)
    hits = chosen_ids[:, :, None] == expert_iota
    row_hits = jnp.sum(hits.astype(jnp.int32), axis=1)
    ranks = jnp.cumsum(row_hits, axis=0) - row_hits
    slot_of = jnp.sum(jnp.where(hits, ranks[:, None, :] + expert_iota * slots_cap, 0), axis=2)
    slot_iota = lax.broadcasted_iota(jnp.int32, (1, 1, experts_all * slots_cap), 2)
    weight_map = jnp.sum(
        jnp.where(slot_of[:, :, None] == slot_iota, chosen_gates[:, :, None], 0.0), axis=1
    )
    return (row_hits, ranks, weight_map)


def body(
    query,
    key_cache_table,
    value_cache_table,
    latest_key,
    latest_value,
    lengths,
    resid,
    norm_gain,
    out_weight,
    expert_ids,
    gate_weights,
    w_gate,
    w_up,
    w_down,
):
    tok_ranks = lax.axis_size("tok")
    tok_place = lax.axis_index("tok")
    exp_ranks = lax.axis_size("exp")
    exp_place = lax.axis_index("exp")
    sub_ranks = lax.axis_size("sub")
    sub_place = lax.axis_index("sub")
    sequence_total = query.shape[2]
    local_extent = key_cache_table.shape[3]
    feature_cols = resid.shape[3]
    query_group_width = QUERY_HEADS // KEY_VALUE_HEADS
    own_heads = QUERY_HEADS // tok_ranks
    score_scale = HEAD_DIMENSION ** (-0.5)
    query_rows = query.reshape(sequence_total, KEY_VALUE_HEADS, query_group_width, HEAD_DIMENSION)
    stored_keys = key_cache_table.reshape(
        sequence_total, local_extent, KEY_VALUE_HEADS, HEAD_DIMENSION
    )
    stored_values = value_cache_table.reshape(
        sequence_total, local_extent, KEY_VALUE_HEADS, HEAD_DIMENSION
    )
    scores = (
        jnp.einsum("rhgd,rphd->rhgp", query_rows, stored_keys, preferred_element_type=jnp.float32)
        * score_scale
    )
    position = tok_place * local_extent + lax.broadcasted_iota(
        jnp.int32, (sequence_total, 1, 1, local_extent), 3
    )
    usable = position < lengths.reshape(sequence_total, 1, 1, 1)
    masked = jnp.where(usable, scores, -1e30)
    block_max = jnp.max(masked, axis=3)
    weights = jnp.where(usable, jnp.exp(masked - block_max[..., None]), 0.0).astype(jnp.bfloat16)
    totals = jnp.sum(weights.astype(jnp.float32), axis=3)
    numerator = jnp.einsum(
        "rhgp,rphd->rhgd", weights, stored_values, preferred_element_type=jnp.float32
    )
    partial_value = (
        (numerator / jnp.maximum(totals, 1.0)[..., None])
        .astype(jnp.bfloat16)
        .reshape(sequence_total, 1, QUERY_HEADS, HEAD_DIMENSION)
    )
    arrived_parts = lax.all_to_all(partial_value, "tok", split_axis=2, concat_axis=1, tiled=True)
    arrived_max, arrived_tot = (
        lax.all_to_all(
            block_max.reshape(sequence_total, 1, QUERY_HEADS),
            "tok",
            split_axis=2,
            concat_axis=1,
            tiled=True,
        ),
        lax.all_to_all(
            totals.reshape(sequence_total, 1, QUERY_HEADS),
            "tok",
            split_axis=2,
            concat_axis=1,
            tiled=True,
        ),
    )
    head_ids = tok_place * own_heads + lax.broadcasted_iota(jnp.int32, (own_heads,), 0)
    key_value_choice = head_ids // query_group_width
    own_query = lax.dynamic_slice_in_dim(
        query.reshape(sequence_total, QUERY_HEADS, HEAD_DIMENSION),
        tok_place * own_heads,
        own_heads,
        1,
    )
    incoming_key = jnp.take(
        latest_key.reshape(sequence_total, KEY_VALUE_HEADS, HEAD_DIMENSION),
        key_value_choice,
        axis=1,
    )
    incoming_value = jnp.take(
        latest_value.reshape(sequence_total, KEY_VALUE_HEADS, HEAD_DIMENSION),
        key_value_choice,
        axis=1,
    )
    own_score = (
        jnp.sum(own_query.astype(jnp.float32) * incoming_key.astype(jnp.float32), axis=2)
        * score_scale
    )
    top_score = jnp.maximum(jnp.max(arrived_max, axis=1), own_score)
    factor = arrived_tot * jnp.exp(arrived_max - top_score[:, None, :])
    self_weight = jnp.exp(own_score - top_score)
    combined = jnp.einsum("rbm,rbmd->rmd", factor, arrived_parts.astype(jnp.float32)) + self_weight[
        ..., None
    ] * incoming_value.astype(jnp.float32)
    heads_out = (
        (combined / (jnp.sum(factor, axis=1) + self_weight)[..., None])
        .reshape(sequence_total, own_heads * HEAD_DIMENSION)
        .astype(jnp.bfloat16)
    )
    attended = lax.psum_scatter(
        lax.dot_general(
            out_weight, heads_out, (((0,), (1,)), ((), ())), preferred_element_type=jnp.float32
        ),
        "tok",
        scatter_dimension=0,
        tiled=True,
    ).T
    hidden_part = resid.reshape(sequence_total, feature_cols).astype(jnp.float32) + attended
    hidden_full = lax.all_gather(hidden_part, "tok", axis=1, tiled=True)
    normed = (
        hidden_full
        * lax.rsqrt(jnp.mean(hidden_full * hidden_full, axis=1, keepdims=True) + 1e-06)
        * norm_gain
    ).astype(jnp.bfloat16)
    source_rows = lax.all_gather(
        normed.reshape(1, sequence_total, D), ("exp", "sub"), axis=0, tiled=True
    ).reshape(-1, D)
    rows_total = exp_ranks * sub_ranks * sequence_total
    experts_all = tok_ranks * sub_ranks
    slots_cap = min(rows_total, max(2, 2 * rows_total * TOPK // experts_all))
    block_cols = D // (tok_ranks * exp_ranks * sub_ranks)
    chosen_ids = jnp.transpose(expert_ids, (1, 0, 2, 3)).reshape(rows_total, TOPK)
    chosen_gates = jnp.transpose(gate_weights, (1, 0, 2, 3)).reshape(rows_total, TOPK)
    row_hits, ranks, weight_map = slot_table(chosen_ids, chosen_gates, experts_all, slots_cap)
    my_expert = tok_place * sub_ranks + sub_place
    my_hits = lax.dynamic_slice_in_dim(row_hits, my_expert, 1, 1)
    my_ranks = lax.dynamic_slice_in_dim(ranks, my_expert, 1, 1)
    slot_iota = lax.broadcasted_iota(jnp.int32, (1, slots_cap), 1)
    picker = ((my_ranks == slot_iota) & (my_hits > 0)).astype(jnp.bfloat16)
    picked = lax.dot_general(
        picker, source_rows, (((0,), (0,)), ((), ())), preferred_element_type=jnp.float32
    ).astype(jnp.bfloat16)
    gate_proj = jnp.dot(picked, w_gate[0], preferred_element_type=jnp.float32)
    up_proj = jnp.dot(picked, w_up[0], preferred_element_type=jnp.float32)
    active = (jax.nn.silu(gate_proj) * up_proj).astype(jnp.bfloat16)
    slice_out = jnp.dot(active, w_down[0], preferred_element_type=jnp.float32)
    summed = lax.psum(slice_out, "exp").astype(jnp.bfloat16)
    mine = lax.dynamic_slice_in_dim(
        summed.reshape(slots_cap, tok_ranks, exp_ranks, sub_ranks, block_cols), exp_place, 1, 2
    )
    expert_y = mine.reshape(slots_cap, tok_ranks * sub_ranks, block_cols)
    received = lax.all_to_all(expert_y, ("tok", "sub"), split_axis=1, concat_axis=0, tiled=True)
    received = (
        lax.optimization_barrier(received)
        .astype(jnp.float32)
        .reshape(experts_all * slots_cap, block_cols)
    )
    mixed = jnp.dot(weight_map, received, precision=lax.Precision.HIGHEST)
    expert_mix = jnp.transpose(
        mixed.reshape(exp_ranks, sub_ranks, sequence_total, block_cols), (1, 0, 2, 3)
    )
    return (attended.reshape(1, 1, sequence_total, feature_cols), expert_mix)


def solution(mesh):
    placed = (
        P(("groups", "sub"), "exp", None, None),
        P(("groups", "sub"), "exp", None, "tok", None),
        P(("groups", "sub"), "exp", None, "tok", None),
        P(("groups", "sub"), "exp", None, None),
        P(("groups", "sub"), "exp", None, None),
        P(("groups", "sub"), "exp", None),
        P(("groups", "sub"), "exp", None, "tok"),
        P(),
        P("tok", None),
        P("groups", None, None, None),
        P("groups", None, None, None),
        P(("tok", "sub"), None, "exp"),
        P(("tok", "sub"), None, "exp"),
        P(("tok", "sub"), "exp", None),
    )
    return jax.shard_map(
        body,
        mesh=mesh,
        in_specs=placed,
        out_specs=(
            P(("groups", "sub"), "exp", None, "tok"),
            P("groups", None, None, ("tok", "exp", "sub")),
        ),
        check_vma=False,
    )
```

profile of v0, /device:TPU:0, one launch (start us, length us, event | category | flops | bytes accessed | tf_op | source)
XLA Modules:
  0.0 179.8 jit_solution(13984810057513307680)
XLA Ops:
  7.2 1.3 reshape.165
  8.6 0.7 broadcast_compare_fusion
  9.3 1.2 fusion.51
  10.5 0.7 copy.79
  11.2 7.3 %all-to-all-start.1 = ((f32[4,1,32]{0,1,2:T(1,128)}), f32[4,1,32]{0,1,2:T(1,128)S(1)}, u32[]{:S(2)}, u32[]{:S(2)}) async-start(f32[4,1,32]{0,1,2:T(1,128)} %bitcast.3), calls=%async_computation.1 | async-start | bytes 32768 | tf_op jit(solution)/shard_map/all_to_all | solution.py:83
  18.6 0.2 convert_reduce_fusion.1
  18.8 0.1 reshape.170
  19.0 0.1 convert_reduce_fusion
  19.1 0.6 gather_fusion
  19.7 0.3 fusion.8
  20.0 0.9 multiply_reduce_fusion.1
  20.8 0.7 copy.77
  21.6 0.6 copy.65
  22.3 0.6 gather_fusion.1
  22.8 2.3 %all-to-all-done.1 = f32[4,1,32]{0,1,2:T(1,128)S(1)} async-done(((f32[4,1,32]{0,1,2:T(1,128)}), f32[4,1,32]{0,1,2:T(1,128)S(1)}, u32[]{:S(2)}, u32[]{:S(2)}) %all-to-all-start.1) | async-done | bytes 544 | tf_op jit(solution)/shard_map/all_to_all | solution.py:83
  25.1 3.7 %all-to-all-start = ((f32[4,1,32]{0,1,2:T(1,128)}), f32[4,1,32]{0,1,2:T(1,128)S(1)}, u32[]{:S(2)}, u32[]{:S(2)}) async-start(f32[4,1,32]{0,1,2:T(1,128)} %bitcast.1), calls=%async_computation | async-start | bytes 32768 | tf_op jit(solution)/shard_map/all_to_all | solution.py:90
  28.9 0.2 dynamic-slice_reduce_fusion
  29.0 0.2 fusion.35
  29.2 0.1 copy.80
  29.4 0.1 copy.84
  29.5 5.9 %all-to-all-done = f32[4,1,32]{0,1,2:T(1,128)S(1)} async-done(((f32[4,1,32]{0,1,2:T(1,128)}), f32[4,1,32]{0,1,2:T(1,128)S(1)}, u32[]{:S(2)}, u32[]{:S(2)}) %all-to-all-start) | async-done | bytes 544 | tf_op jit(solution)/shard_map/all_to_all | solution.py:90
  35.4 3.3 %all-to-all-start.2 = ((bf16[4,1,32,128]{3,0,1,2:T(4,128)(2,1)}), bf16[4,1,32,128]{3,0,1,2:T(4,128)(2,1)S(1)}, u32[]{:S(2)}, u32[]{:S(2)}) async-start(bf16[4,1,32,128]{3,0,1,2:T(4,128)(2,1)} %copy.65), calls=%async_computation.2 | async-start | bytes 65536 | tf_op jit(solution)/shard_map/all_to_all | solution.py:81
  38.8 0.1 copy.78
  39.0 0.1 copy.66
  39.1 0.1 copy.67
  39.2 0.1 copy.73
  39.3 6.1 %all-to-all-done.2 = bf16[4,1,32,128]{3,0,1,2:T(4,128)(2,1)S(1)} async-done(((bf16[4,1,32,128]{3,0,1,2:T(4,128)(2,1)}), bf16[4,1,32,128]{3,0,1,2:T(4,128)(2,1)S(1)}, u32[]{:S(2)}, u32[]{:S(2)}) %all-to-all-start.2) | async-done | bytes 32800 | tf_op jit(solution)/shard_map/all_to_all | solution.py:81
  45.4 0.1 fusion.22
  45.5 0.4 convolution_bitcast_fusion
  46.0 1.4 copy.82
  47.4 0.4 select_reduce_fusion.1
  47.8 61.6 %reduce-scatter.4.cloned.1.call-done = f32[256,4]{1,0:T(8,128)} async-done(((f32[2048,4]{1,0:T(8,128)}), f32[256,4]{1,0:T(8,128)}) %reduce-scatter.4.cloned.1.call-update) | async-done | bytes 4112
  109.4 1.0 copy.83
  110.4 30.6 %all_gather.6 = f32[4,2048]{1,0:T(4,128)S(1)} all-gather(f32[4,256]{1,0:T(4,128)S(1)} %convert_add_fusion), channel_id=1, replica_groups=mesh['groups'=1,'tok'=8,'exp'=2,'sub'=2] {'tok'}, dimensions={1}, use_global_device_ids=true | all-gather | bytes 36864 | tf_op jit(solution)/shard_map/all_gather | solution.py:140
  141.0 0.1 multiply_reduce_fusion
  141.2 5.2 %all-gather.1 = bf16[4,4,2048]{2,1,0:T(4,128)(2,1)S(1)} all-gather(bf16[1,4,2048]{2,1,0:T(4,128)(2,1)S(1)} %fusion.29), channel_id=2, replica_groups=mesh['groups'=1,'tok'=8,'exp'=2,'sub'=2] {'exp','sub'}, dimensions={0}, use_global_device_ids=true | all-gather | bytes 81920 | tf_op jit(solution)/shard_map/all_gather | solution.py:146
  146.5 0.3 convolution_convert_fusion
  146.8 1.7 fusion.4
  148.5 2.6 %fusion = f32[16,2048]{1,0:T(8,128)S(1)} fusion(bf16[1,384,2048]{2,1,0:T(8,128)(2,1)} %param.29, bf16[16,2048]{1,0:T(8,128)(2,1)S(1)} %convolution_convert_fusion, bf16[1,2048,384]{2,1,0:T(8,128)(2,1)} %param.28, f32[16,384]{1,0:T(8,128)S(1)} %fusion.4), kind=kOutput, calls=%fused_computation.4 | convolution fusion | flops 50368512 | bytes 3366912 | tf_op jit(solution)/shard_map/dot_general | solution.py:167
  151.1 9.7 %all-reduce.1 = bf16[16,2048]{1,0:T(8,128)(2,1)S(1)} all-reduce(f32[16,2048]{1,0:T(8,128)S(1)} %fusion), channel_id=1, replica_groups=mesh['groups'=1,'tok'=8,'exp'=2,'sub'=2] {'exp'}, use_global_device_ids=true, to_apply=%region_11.13 | all-reduce | flops 32768 | bytes 196608 | tf_op jit(solution)/shard_map/psum | solution.py:168
  160.9 0.2 reshape.176
  161.2 0.7 reshape.213
  161.9 3.5 %all-to-all-start.3 = ((bf16[16,2,512]{2,1,0:T(2,128)(2,1)}), bf16[16,2,512]{2,1,0:T(2,128)(2,1)S(1)}, u32[]{:S(2)}, u32[]{:S(2)}) async-start(bf16[16,2,512]{2,1,0:T(2,128)(2,1)} %reshape.213), calls=%async_computation.3 | async-start | bytes 65536 | tf_op jit(solution)/shard_map/all_to_all | solution.py:173
  165.4 0.1 select_reduce_fusion
  165.6 6.5 %all-to-all-done.3 = bf16[16,2,512]{2,1,0:T(2,128)(2,1)S(1)} async-done(((bf16[16,2,512]{2,1,0:T(2,128)(2,1)}), bf16[16,2,512]{2,1,0:T(2,128)(2,1)S(1)}, u32[]{:S(2)}, u32[]{:S(2)}) %all-to-all-start.3) | async-done | bytes 32800 | tf_op jit(solution)/shard_map/all_to_all | solution.py:173
  172.1 0.1 reshape.214
  172.2 0.1 convolution_bitcast_fusion.1
  172.3 0.6 copy.72
  (43 shorter events, 0.6 us)
Async XLA Ops:
  7.2 38.4 %copy-start = (bf16[512,2048]{1,0:T(8,128)(2,1)S(1)}, bf16[512,2048]{1,0:T(8,128)(2,1)}, u32[]{:S(2)}) copy-start(bf16[512,2048]{1,0:T(8,128)(2,1)} %param.24) | copy-start | bytes 6291460
  7.2 11.6 %copy-start.1 = (bf16[1,1,4,128,512]{4,3,2,1,0:T(8,128)(2,1)S(1)}, bf16[1,1,4,128,512]{4,3,2,1,0:T(8,128)(2,1)}, u32[]{:S(2)}) copy-start(bf16[1,1,4,128,512]{4,3,2,1,0:T(8,128)(2,1)} %param.18) | copy-start | bytes 1572868
  7.2 11.8 %copy-start.4 = (s32[2,2,4,8]{3,2,1,0:T(4,128)S(1)}, s32[2,2,4,8]{3,2,1,0:T(4,128)}, u32[]{:S(2)}) copy-start(s32[2,2,4,8]{3,2,1,0:T(4,128)} %param.25) | copy-start | bytes 1540
  7.2 11.9 %copy-start.6 = (bf16[1,1,4,512]{3,2,1,0:T(4,128)(2,1)S(1)}, bf16[1,1,4,512]{3,2,1,0:T(4,128)(2,1)}, u32[]{:S(2)}) copy-start(bf16[1,1,4,512]{3,2,1,0:T(4,128)(2,1)} %param.19) | copy-start | bytes 12292
  8.5 13.7 %copy-start.7 = (bf16[1,1,4,512]{3,2,1,0:T(4,128)(2,1)S(1)}, bf16[1,1,4,512]{3,2,1,0:T(4,128)(2,1)}, u32[]{:S(2)}) copy-start(bf16[1,1,4,512]{3,2,1,0:T(4,128)(2,1)} %param.20) | copy-start | bytes 12292
  8.6 20.3 %copy-start.5 = (f32[2,2,4,8]{3,2,1,0:T(4,128)S(1)}, f32[2,2,4,8]{3,2,1,0:T(4,128)}, u32[]{:S(2)}) copy-start(f32[2,2,4,8]{3,2,1,0:T(4,128)} %param.26) | copy-start | bytes 1540
  11.2 13.9 %all-to-all-start.1 = ((f32[4,1,32]{0,1,2:T(1,128)}), f32[4,1,32]{0,1,2:T(1,128)S(1)}, u32[]{:S(2)}, u32[]{:S(2)}) async-start(f32[4,1,32]{0,1,2:T(1,128)} %bitcast.3), calls=%async_computation.1 | async-start | bytes 32768 | tf_op jit(solution)/shard_map/all_to_all | solution.py:83
  25.1 10.3 %all-to-all-start = ((f32[4,1,32]{0,1,2:T(1,128)}), f32[4,1,32]{0,1,2:T(1,128)S(1)}, u32[]{:S(2)}, u32[]{:S(2)}) async-start(f32[4,1,32]{0,1,2:T(1,128)} %bitcast.1), calls=%async_computation | async-start | bytes 32768 | tf_op jit(solution)/shard_map/all_to_all | solution.py:90
  35.4 10.0 %all-to-all-start.2 = ((bf16[4,1,32,128]{3,0,1,2:T(4,128)(2,1)}), bf16[4,1,32,128]{3,0,1,2:T(4,128)(2,1)S(1)}, u32[]{:S(2)}, u32[]{:S(2)}) async-start(bf16[4,1,32,128]{3,0,1,2:T(4,128)(2,1)} %copy.65), calls=%async_computation.2 | async-start | bytes 65536 | tf_op jit(solution)/shard_map/all_to_all | solution.py:81
  38.8 70.7 %reduce-scatter.4.cloned.1.call-start = ((), (), s32[]{:S(2)}) async-start(), calls=%async_computation.5 | async-start | bytes 1179648
  46.0 64.4 %copy-start.8 = (bf16[1,1,4,256]{3,2,1,0:T(4,128)(2,1)S(1)}, bf16[1,1,4,256]{3,2,1,0:T(4,128)(2,1)}, u32[]{:S(2)}) copy-start(bf16[1,1,4,256]{3,2,1,0:T(4,128)(2,1)} %param.22) | copy-start | bytes 6148
  46.0 95.2 %copy-start.3 = (f32[2048]{0:T(1024)S(1)}, f32[2048]{0:T(1024)}, u32[]{:S(2)}) copy-start(f32[2048]{0:T(1024)} %param.23) | copy-start | bytes 24580
  110.4 40.7 %copy-start.2 = (f32[256,4]{0,1:T(4,128)}, f32[256,4]{0,1:T(4,128)S(1)}, u32[]{:S(2)}) copy-start(f32[256,4]{0,1:T(4,128)S(1)} %copy.83) | copy-start | bytes 12292
  161.9 10.2 %all-to-all-start.3 = ((bf16[16,2,512]{2,1,0:T(2,128)(2,1)}), bf16[16,2,512]{2,1,0:T(2,128)(2,1)S(1)}, u32[]{:S(2)}, u32[]{:S(2)}) async-start(bf16[16,2,512]{2,1,0:T(2,128)(2,1)} %reshape.213), calls=%async_computation.3 | async-start | bytes 65536 | tf_op jit(solution)/shard_map/all_to_all | solution.py:173
Sparse Core Ops, SparseCore 0:
  47.5 61.8 reduce-scatter.3
where the time goes:
time: 180 us
  waiting for transfers between devices  82.4 us (46%)
  blocking collectives  45.6 us (25%)
  starting transfers between devices  17.9 us (10%)
  between operations  14.3 us (8%)
  local copies, waits for them, and re-layouts  9.66 us (5%)
  matrix products  6.85 us (4%)
  other arithmetic  2.97 us (2%)
    unnamed x2, waiting for transfers between devices  61.7 us
    all_gather x1, blocking collectives, body(): hidden_full = lax.all_gather(hidden_part, 'tok', axis=1, tiled=True)  30.6 us
    psum x1, blocking collectives, body(): summed = lax.psum(slice_out, 'exp').astype(jnp.bfloat16)  9.75 us
    all_to_all x1, starting transfers between devices, body(): lax.all_to_all(block_max.reshape(sequence_total, 1, QUERY_HEADS), 'tok',...  7.31 us
    all_to_all x1, waiting for transfers between devices, body(): lax.all_to_all(expert_y, ('tok', 'sub'), split_axis=1, concat_axis=0, til...  6.49 us
    all_to_all x1, waiting for transfers between devices, body(): lax.all_to_all(partial_value, 'tok', split_axis=2, concat_axis=1, tiled=T...  6.05 us
    all_to_all x1, waiting for transfers between devices, body(): lax.all_to_all(totals.reshape(sequence_total, 1, QUERY_HEADS), 'tok', spl...  5.94 us
    all_gather x1, blocking collectives, body(): lax.all_gather(normed.reshape(1, sequence_total, D), ('exp', 'sub'), axis...  5.23 us
  transfers between devices with their start and end apart: 5, of which 5 were waited for; matrix products, arithmetic and copies ran while one was open for 3% of the time, Pallas kernels for 0%

commit v1 on v0

--- a/solution.py
+++ b/solution.py
@@ -79,6 +79,19 @@
         .reshape(sequence_total, 1, QUERY_HEADS, HEAD_DIMENSION)
     )
     arrived_parts = lax.all_to_all(partial_value, "tok", split_axis=2, concat_axis=1, tiled=True)
+
+    def try_all_lots_all(inp):
+        front = jnp.concatenate(
+            lax.all_to_all(
+                jnp.stack(jnp.split(inp, lax.axis_size("tok"), axis=2)),
+                "tok",
+                split_axis=0,
+                concat_axis=0,
+            ),
+            axis=1,
+        )
+        return front
+
     arrived_max, arrived_tot = (
         lax.all_to_all(
             block_max.reshape(sequence_total, 1, QUERY_HEADS),
@@ -87,13 +100,7 @@
             concat_axis=1,
             tiled=True,
         ),
-        lax.all_to_all(
-            totals.reshape(sequence_total, 1, QUERY_HEADS),
-            "tok",
-            split_axis=2,
-            concat_axis=1,
-            tiled=True,
-        ),
+        try_all_lots_all(totals.reshape(sequence_total, 1, QUERY_HEADS)),
     )
     head_ids = tok_place * own_heads + lax.broadcasted_iota(jnp.int32, (own_heads,), 0)
     key_value_choice = head_ids // query_group_width

time: 180 us -> 185 us (1.028)
  local copies, waits for them, and re-layouts: 9.66 us -> 14 us
    unnamed x26 -> x33, local copies, waits for them, and re-layouts: 3.94 us -> 8.45 us
    all_to_all x1, starting transfers between devices: 7.31 us -> 3.53 us  [body(): lax.all_to_all(block_max.reshape(sequence_total, 1, QUERY_HEADS), 'tok',...]
    all_to_all x1, waiting for transfers between devices: 2.3 us -> 6.08 us  [body(): lax.all_to_all(block_max.reshape(sequence_total, 1, QUERY_HEADS), 'tok',...]
    all_to_all x1, starting transfers between devices: 3.72 us -> 7.31 us  [try_all_lots_all(): lax.all_to_all(jnp.stack(jnp.split(inp, lax.axis_size('tok'), axis=2)), '...]
    all_to_all x1, waiting for transfers between devices: 5.94 us -> 2.49 us  [try_all_lots_all(): lax.all_to_all(jnp.stack(jnp.split(inp, lax.axis_size('tok'), axis=2)), '...]
where the time goes in v1:
time: 185 us; the launch traced here: 184 us
  waiting for transfers between devices  82.7 us (45%)
  blocking collectives  45.6 us (25%)
  starting transfers between devices  17.8 us (10%)
  between operations  14.3 us (8%)
  local copies, waits for them, and re-layouts  14 us (8%)
  matrix products  6.86 us (4%)
  other arithmetic  3.12 us (2%)
    unnamed x2, waiting for transfers between devices  61.7 us
    all_gather x1, blocking collectives, body(): hidden_full = lax.all_gather(hidden_part, 'tok', axis=1, tiled=True)  30.6 us
    psum x1, blocking collectives, body(): summed = lax.psum(slice_out, 'exp').astype(jnp.bfloat16)  9.75 us
    unnamed x33, local copies, waits for them, and re-layouts  8.45 us
    all_to_all x1, starting transfers between devices, try_all_lots_all(): lax.all_to_all(jnp.stack(jnp.split(inp, lax.axis_size('tok'), axis=2)), '...  7.31 us
    all_to_all x1, waiting for transfers between devices, body(): lax.all_to_all(expert_y, ('tok', 'sub'), split_axis=1, concat_axis=0, til...  6.49 us
    all_to_all x1, waiting for transfers between devices, body(): lax.all_to_all(block_max.reshape(sequence_total, 1, QUERY_HEADS), 'tok',...  6.08 us
    all_to_all x1, waiting for transfers between devices, body(): lax.all_to_all(partial_value, 'tok', split_axis=2, concat_axis=1, tiled=T...  5.98 us
  transfers between devices with their start and end apart: 5, of which 5 were waited for; matrix products, arithmetic and copies ran while one was open for 3% of the time, Pallas kernels for 0%

profile of v1, /device:TPU:0, one launch (start us, length us, event | category | flops | bytes accessed | tf_op | source)
XLA Modules:
  0.0 184.4 jit_solution(6295038804937707798)
XLA Ops:
  7.2 1.3 reshape.165
  8.6 0.7 broadcast_compare_fusion
  9.3 1.2 fusion.50
  10.5 0.2 convert_reduce_fusion.1
  10.8 0.6 constant_dynamic-update-slice_fusion.7
  11.4 0.7 constant_dynamic-update-slice_fusion.6
  12.1 0.6 constant_dynamic-update-slice_fusion.5
  12.7 0.7 constant_dynamic-update-slice_fusion.4
  13.4 0.7 constant_dynamic-update-slice_fusion.3
  14.0 0.6 constant_dynamic-update-slice_fusion.2
  14.7 0.7 constant_dynamic-update-slice_fusion.1
  15.3 0.6 constant_dynamic-update-slice_fusion
  16.0 7.3 %all-to-all-start = ((f32[8,4,1,4]{3,1,2,0:T(4,128)}), f32[8,4,1,4]{3,1,2,0:T(4,128)S(1)}, u32[]{:S(2)}, u32[]{:S(2)}) async-start(f32[8,4,1,4]{3,1,2,0:T(4,128)} %constant_dynamic-update-slice_fusion), calls=%async_computation | async-start | bytes 32768 | tf_op jit(solution)/shard_map/all_to_all | solution.py:85
  23.3 0.1 reshape.172
  23.6 0.6 gather_fusion
  24.2 0.3 fusion.8
  24.5 0.9 multiply_reduce_fusion.1
  25.4 0.7 copy.81
  26.2 0.6 copy.69
  26.8 0.6 gather_fusion.1
  27.4 2.5 %all-to-all-done = f32[8,4,1,4]{3,1,2,0:T(4,128)S(1)} async-done(((f32[8,4,1,4]{3,1,2,0:T(4,128)}), f32[8,4,1,4]{3,1,2,0:T(4,128)S(1)}, u32[]{:S(2)}, u32[]{:S(2)}) %all-to-all-start) | async-done | bytes 544 | tf_op jit(solution)/shard_map/all_to_all | solution.py:85
  29.8 3.5 %all-to-all-start.1 = ((f32[4,1,32]{0,1,2:T(1,128)}), f32[4,1,32]{0,1,2:T(1,128)S(1)}, u32[]{:S(2)}, u32[]{:S(2)}) async-start(f32[4,1,32]{0,1,2:T(1,128)} %bitcast.11), calls=%async_computation.1 | async-start | bytes 32768 | tf_op jit(solution)/shard_map/all_to_all | solution.py:96
  33.4 0.2 dynamic-slice_reduce_fusion
  33.6 0.2 fusion.35
  33.9 6.1 %all-to-all-done.1 = f32[4,1,32]{0,1,2:T(1,128)S(1)} async-done(((f32[4,1,32]{0,1,2:T(1,128)}), f32[4,1,32]{0,1,2:T(1,128)S(1)}, u32[]{:S(2)}, u32[]{:S(2)}) %all-to-all-start.1) | async-done | bytes 544 | tf_op jit(solution)/shard_map/all_to_all | solution.py:96
  39.9 3.3 %all-to-all-start.2 = ((bf16[4,1,32,128]{3,0,1,2:T(4,128)(2,1)}), bf16[4,1,32,128]{3,0,1,2:T(4,128)(2,1)S(1)}, u32[]{:S(2)}, u32[]{:S(2)}) async-start(bf16[4,1,32,128]{3,0,1,2:T(4,128)(2,1)} %copy.69), calls=%async_computation.2 | async-start | bytes 65536 | tf_op jit(solution)/shard_map/all_to_all | solution.py:81
  43.6 0.2 fusion.49
  43.9 6.0 %all-to-all-done.2 = bf16[4,1,32,128]{3,0,1,2:T(4,128)(2,1)S(1)} async-done(((bf16[4,1,32,128]{3,0,1,2:T(4,128)(2,1)}), bf16[4,1,32,128]{3,0,1,2:T(4,128)(2,1)S(1)}, u32[]{:S(2)}, u32[]{:S(2)}) %all-to-all-start.2) | async-done | bytes 32800 | tf_op jit(solution)/shard_map/all_to_all | solution.py:81
  49.9 0.1 fusion.22
  50.0 0.4 convolution_bitcast_fusion
  50.5 1.4 copy.85
  51.9 0.4 select_reduce_fusion.1
  52.3 61.7 %reduce-scatter.4.cloned.1.call-done = f32[256,4]{1,0:T(8,128)} async-done(((f32[2048,4]{1,0:T(8,128)}), f32[256,4]{1,0:T(8,128)}) %reduce-scatter.4.cloned.1.call-update) | async-done | bytes 4112
  114.0 1.0 copy.86
  115.0 30.6 %all_gather.6 = f32[4,2048]{1,0:T(4,128)S(1)} all-gather(f32[4,256]{1,0:T(4,128)S(1)} %convert_add_fusion), channel_id=1, replica_groups=mesh['groups'=1,'tok'=8,'exp'=2,'sub'=2] {'tok'}, dimensions={1}, use_global_device_ids=true | all-gather | bytes 36864 | tf_op jit(solution)/shard_map/all_gather | solution.py:147
  145.6 0.1 multiply_reduce_fusion
  145.8 5.2 %all-gather.1 = bf16[4,4,2048]{2,1,0:T(4,128)(2,1)S(1)} all-gather(bf16[1,4,2048]{2,1,0:T(4,128)(2,1)S(1)} %fusion.29), channel_id=2, replica_groups=mesh['groups'=1,'tok'=8,'exp'=2,'sub'=2] {'exp','sub'}, dimensions={0}, use_global_device_ids=true | all-gather | bytes 81920 | tf_op jit(solution)/shard_map/all_gather | solution.py:153
  151.1 0.3 convolution_convert_fusion
  151.3 1.7 fusion.4
  153.1 2.6 %fusion = f32[16,2048]{1,0:T(8,128)S(1)} fusion(bf16[1,384,2048]{2,1,0:T(8,128)(2,1)} %param.29, bf16[16,2048]{1,0:T(8,128)(2,1)S(1)} %convolution_convert_fusion, bf16[1,2048,384]{2,1,0:T(8,128)(2,1)} %param.28, f32[16,384]{1,0:T(8,128)S(1)} %fusion.4), kind=kOutput, calls=%fused_computation.4 | convolution fusion | flops 50368512 | bytes 3366912 | tf_op jit(solution)/shard_map/dot_general | solution.py:174
  155.7 9.7 %all-reduce.1 = bf16[16,2048]{1,0:T(8,128)(2,1)S(1)} all-reduce(f32[16,2048]{1,0:T(8,128)S(1)} %fusion), channel_id=1, replica_groups=mesh['groups'=1,'tok'=8,'exp'=2,'sub'=2] {'exp'}, use_global_device_ids=true, to_apply=%region_11.13 | all-reduce | flops 32768 | bytes 196608 | tf_op jit(solution)/shard_map/psum | solution.py:175
  165.4 0.2 reshape.178
  165.7 0.7 reshape.215
  166.4 3.6 %all-to-all-start.3 = ((bf16[16,2,512]{2,1,0:T(2,128)(2,1)}), bf16[16,2,512]{2,1,0:T(2,128)(2,1)S(1)}, u32[]{:S(2)}, u32[]{:S(2)}) async-start(bf16[16,2,512]{2,1,0:T(2,128)(2,1)} %reshape.215), calls=%async_computation.3 | async-start | bytes 65536 | tf_op jit(solution)/shard_map/all_to_all | solution.py:180
  170.0 0.1 select_reduce_fusion
  170.2 6.5 %all-to-all-done.3 = bf16[16,2,512]{2,1,0:T(2,128)(2,1)S(1)} async-done(((bf16[16,2,512]{2,1,0:T(2,128)(2,1)}), bf16[16,2,512]{2,1,0:T(2,128)(2,1)S(1)}, u32[]{:S(2)}, u32[]{:S(2)}) %all-to-all-start.3) | async-done | bytes 32800 | tf_op jit(solution)/shard_map/all_to_all | solution.py:180
  176.8 0.1 convolution_bitcast_fusion.1
  176.9 0.6 copy.76
  (49 shorter events, 1.3 us)
Async XLA Ops:
  7.2 42.9 %copy-start = (bf16[512,2048]{1,0:T(8,128)(2,1)S(1)}, bf16[512,2048]{1,0:T(8,128)(2,1)}, u32[]{:S(2)}) copy-start(bf16[512,2048]{1,0:T(8,128)(2,1)} %param.24) | copy-start | bytes 6291460
  7.2 16.2 %copy-start.1 = (bf16[1,1,4,128,512]{4,3,2,1,0:T(8,128)(2,1)S(1)}, bf16[1,1,4,128,512]{4,3,2,1,0:T(8,128)(2,1)}, u32[]{:S(2)}) copy-start(bf16[1,1,4,128,512]{4,3,2,1,0:T(8,128)(2,1)} %param.18) | copy-start | bytes 1572868
  7.2 16.3 %copy-start.4 = (s32[2,2,4,8]{3,2,1,0:T(4,128)S(1)}, s32[2,2,4,8]{3,2,1,0:T(4,128)}, u32[]{:S(2)}) copy-start(s32[2,2,4,8]{3,2,1,0:T(4,128)} %param.25) | copy-start | bytes 1540
  7.2 16.4 %copy-start.6 = (bf16[1,1,4,512]{3,2,1,0:T(4,128)(2,1)S(1)}, bf16[1,1,4,512]{3,2,1,0:T(4,128)(2,1)}, u32[]{:S(2)}) copy-start(bf16[1,1,4,512]{3,2,1,0:T(4,128)(2,1)} %param.19) | copy-start | bytes 12292
  8.6 18.2 %copy-start.7 = (bf16[1,1,4,512]{3,2,1,0:T(4,128)(2,1)S(1)}, bf16[1,1,4,512]{3,2,1,0:T(4,128)(2,1)}, u32[]{:S(2)}) copy-start(bf16[1,1,4,512]{3,2,1,0:T(4,128)(2,1)} %param.20) | copy-start | bytes 12292
  8.6 24.8 %copy-start.5 = (f32[2,2,4,8]{3,2,1,0:T(4,128)S(1)}, f32[2,2,4,8]{3,2,1,0:T(4,128)}, u32[]{:S(2)}) copy-start(f32[2,2,4,8]{3,2,1,0:T(4,128)} %param.26) | copy-start | bytes 1540
  16.0 13.9 %all-to-all-start = ((f32[8,4,1,4]{3,1,2,0:T(4,128)}), f32[8,4,1,4]{3,1,2,0:T(4,128)S(1)}, u32[]{:S(2)}, u32[]{:S(2)}) async-start(f32[8,4,1,4]{3,1,2,0:T(4,128)} %constant_dynamic-update-slice_fusion), calls=%async_computation | async-start | bytes 32768 | tf_op jit(solution)/shard_map/all_to_all | solution.py:85
  29.8 10.1 %all-to-all-start.1 = ((f32[4,1,32]{0,1,2:T(1,128)}), f32[4,1,32]{0,1,2:T(1,128)S(1)}, u32[]{:S(2)}, u32[]{:S(2)}) async-start(f32[4,1,32]{0,1,2:T(1,128)} %bitcast.11), calls=%async_computation.1 | async-start | bytes 32768 | tf_op jit(solution)/shard_map/all_to_all | solution.py:96
  39.9 10.0 %all-to-all-start.2 = ((bf16[4,1,32,128]{3,0,1,2:T(4,128)(2,1)}), bf16[4,1,32,128]{3,0,1,2:T(4,128)(2,1)S(1)}, u32[]{:S(2)}, u32[]{:S(2)}) async-start(bf16[4,1,32,128]{3,0,1,2:T(4,128)(2,1)} %copy.69), calls=%async_computation.2 | async-start | bytes 65536 | tf_op jit(solution)/shard_map/all_to_all | solution.py:81
  43.3 70.7 %reduce-scatter.4.cloned.1.call-start = ((), (), s32[]{:S(2)}) async-start(), calls=%async_computation.5 | async-start | bytes 1179648
  50.5 64.5 %copy-start.8 = (bf16[1,1,4,256]{3,2,1,0:T(4,128)(2,1)S(1)}, bf16[1,1,4,256]{3,2,1,0:T(4,128)(2,1)}, u32[]{:S(2)}) copy-start(bf16[1,1,4,256]{3,2,1,0:T(4,128)(2,1)} %param.22) | copy-start | bytes 6148
  50.5 95.2 %copy-start.3 = (f32[2048]{0:T(1024)S(1)}, f32[2048]{0:T(1024)}, u32[]{:S(2)}) copy-start(f32[2048]{0:T(1024)} %param.23) | copy-start | bytes 24580
  114.9 40.7 %copy-start.2 = (f32[256,4]{0,1:T(4,128)}, f32[256,4]{0,1:T(4,128)S(1)}, u32[]{:S(2)}) copy-start(f32[256,4]{0,1:T(4,128)S(1)} %copy.86) | copy-start | bytes 12292
  166.4 10.2 %all-to-all-start.3 = ((bf16[16,2,512]{2,1,0:T(2,128)(2,1)}), bf16[16,2,512]{2,1,0:T(2,128)(2,1)S(1)}, u32[]{:S(2)}, u32[]{:S(2)}) async-start(bf16[16,2,512]{2,1,0:T(2,128)(2,1)} %reshape.215), calls=%async_computation.3 | async-start | bytes 65536 | tf_op jit(solution)/shard_map/all_to_all | solution.py:180
Sparse Core Ops, SparseCore 0:
  52.0 61.9 reduce-scatter.3
